TPU v7x, 32 devices: a whole 2x2x4 slice. The times are simulated.
32 devices in a mesh: grp: 2 (over y), seq: 4 (over z), sub: 4 (over x, core).
Axes of the slice: x: 2, y: 2, z: 4, core: 2. Of those that a mesh axis runs over, the one named last changes fastest.
Arguments:
- activations: bfloat16 [32768, 384], P(('grp', 'seq', 'sub')), parts along dimension 0, may hold values from -6 to 6
- cotangent: bfloat16 [32768, 384], P(('grp', 'seq', 'sub')), parts along dimension 0, may hold values from -6 to 6
- weights: bfloat16 [2304, 384], P('sub'), may hold values from -0.1875 to 0.1875
Outputs:
- input_grad: bfloat16 [32768, 384], P(('grp', 'seq', 'sub')), parts along dimension 0
- weight_grad: float32 [4608, 384], P(('grp', 'sub')), parts along dimension 0
There are 2 independent parts, one for each index of `grp`. A program takes and returns all parts, laid end to end along the dimension named above; an argument that names none is the same for every part. Nothing has to cross between parts.
All inputs are finite; a program needn't handle non-finite values.
Results may differ from a plain program's by a relative error of at most 0.0053.
Values may be sent and summed in bfloat16 or wider, within the bound.
No kernel may reach another device: no remote copies, remote signals or barrier semaphores. Data moves between devices by JAX's collectives and lax.ppermute only.
A program may use at most 64 MiB of HBM per device.

v0:
```python
import math
import jax
import jax.numpy as jnp
from jax import lax
from jax.sharding import PartitionSpec as P

DILATION_FIRST = 1024
DILATION_SECOND = 2048


def from_behind(block, axis, distance):
    devices = range(lax.axis_size(axis))
    route = [(i - distance, i) for i in devices if i - distance in devices]
    return lax.ppermute(block, axis, route)


def gelu_pair(pre_act):
    coeff = 0.7978845608
    tanh_value = jnp.tanh(coeff * (pre_act + 0.044715 * pre_act * pre_act * pre_act))
    gelu_value = 0.5 * pre_act * (1.0 + tanh_value)
    gelu_slope = 0.5 * (1.0 + tanh_value) + 0.5 * pre_act * (
        1.0 - tanh_value * tanh_value
    ) * coeff * (1.0 + 3.0 * 0.044715 * pre_act * pre_act)
    return (gelu_value, gelu_slope)


def back_product(spread, kernel, count_of_rows, channels):
    spread_three = spread.reshape(count_of_rows, 3, channels)
    kernel_three = kernel.reshape(3, channels, channels)
    return lax.dot_general(
        spread_three, kernel_three, (((1, 2), (0, 2)), ((), ())), preferred_element_type=jnp.float32
    )


def tap_grads(stacked, delta):
    return lax.dot_general(
        stacked, delta, (((0,), (0,)), ((), ())), preferred_element_type=jnp.float32
    )


def per_device(activations, cotangent, weights):
    count_of_rows, channels = activations.shape
    devices = lax.axis_size("seq") * lax.axis_size("sub")
    nearby_jumps = DILATION_FIRST // count_of_rows
    distant_jumps = DILATION_SECOND // count_of_rows
    grad_scale = 1.0 / math.sqrt(count_of_rows * devices)
    all_weights = lax.all_gather(weights, "sub", axis=0, tiled=True)
    first = all_weights[: 3 * channels]
    second = all_weights[3 * channels :]

    def near_rows(source, sign):
        return from_behind(source, ("seq", "sub"), sign * nearby_jumps)

    def far_rows(source, sign):
        return from_behind(source, ("seq", "sub"), sign * distant_jumps)

    first_layer_weights = jnp.concatenate(
        (near_rows(activations, 1), activations, near_rows(activations, -1)), 1
    )
    pre_one = jnp.dot(first_layer_weights, first, preferred_element_type=jnp.float32)
    gelu_one, slope_one = gelu_pair(pre_one)
    middle_state = (activations.astype(jnp.float32) + gelu_one).astype(jnp.bfloat16)
    second_layer_weights = jnp.concatenate(
        (far_rows(middle_state, 1), middle_state, far_rows(middle_state, -1)), 1
    )
    pre_two = jnp.dot(second_layer_weights, second, preferred_element_type=jnp.float32)
    gelu_two, slope_two = gelu_pair(pre_two)
    second_error = (cotangent.astype(jnp.float32) * slope_two).astype(jnp.bfloat16)
    grad_two = tap_grads(second_layer_weights, second_error) * grad_scale
    second_reach = jnp.concatenate(
        (far_rows(second_error, -1), second_error, far_rows(second_error, 1)), 1
    )
    back_one = cotangent.astype(jnp.float32) + back_product(
        second_reach, second, count_of_rows, channels
    )
    first_error = (back_one * slope_one).astype(jnp.bfloat16)
    grad_one = tap_grads(first_layer_weights, first_error) * grad_scale
    first_reach = jnp.concatenate(
        (near_rows(first_error, -1), first_error, near_rows(first_error, 1)), 1
    )
    input_grad = (back_one + back_product(first_reach, first, count_of_rows, channels)).astype(
        jnp.bfloat16
    )
    local_grads = jnp.concatenate((grad_one, grad_two), 0)
    summed = lax.psum(local_grads, "seq")
    weight_grad = lax.psum_scatter(summed, "sub", scatter_dimension=0, tiled=True)
    return (input_grad, weight_grad)


def solution(mesh):
    placed = (P(("grp", "seq", "sub"), None), P(("grp", "seq", "sub"), None), P("sub", None))
    return jax.shard_map(
        per_device,
        mesh=mesh,
        in_specs=placed,
        out_specs=(P(("grp", "seq", "sub"), None), P(("grp", "sub"), None)),
        check_vma=False,
    )
```

profile of v0, /device:TPU:0, one launch (start us, length us, event | category | flops | bytes accessed | tf_op | source)
XLA Modules:
  0.0 237.5 jit_solution(14820011768576403430)
XLA Ops:
  8.0 2.4 %collective-permute-start = (bf16[1024,384]{1,0:T(8,128)(2,1)}, bf16[1024,384]{1,0:T(8,128)(2,1)S(1)}, u32[]{:S(2)}, u32[]{:S(2)}) collective-permute-start(bf16[1024,384]{1,0:T(8,128)(2,1)} %param.3), channel_id=1, source_target_pairs={{0,1},{1,2},{2,3},{3,4},{4,5},{5,6},{6,7},{7,8},{8,9},{9,10},{10,1... | collective-permute-start | bytes 2359304 | tf_op jit(solution)/shard_map/ppermute | solution.py:14
  10.4 1.3 collective-permute-start.1
  11.7 1.4 copy.6
  15.1 1.7 collective-permute-done.1
  17.8 22.2 %all-gather.2.cloned.1.call-done = bf16[2304,384]{1,0:T(8,128)(2,1)} async-done(((bf16[576,384]{1,0:T(8,128)(2,1)}), bf16[2304,384]{1,0:T(8,128)(2,1)}) %all-gather.2.cloned.1.call-update) | async-done | bytes 1769488 | tf_op jit(solution)/shard_map/all_gather | solution.py:47
  40.0 4.9 %add_convert_fusion = (bf16[1024,384]{0,1:T(8,128)(2,1)}, f32[1024,384]{0,1:T(8,128)}) fusion(bf16[1024,384]{0,1:T(8,128)(2,1)S(1)} %copy.6, bf16[1024,1152]{1,0:T(8,128)(2,1)} %constant_dynamic-update-slice_fusion, bf16[2304,384]{1,0:T(8,128)(2,1)} %all-gather.2.cloned.1.call-done), kind=kOutput, calls=%fused_computation.27 | convolution fusion | flops 910295040 | bytes 6389760 | tf_op jit(solution)/shard_map/dot_general | solution.py:60
  44.9 1.3 collective-permute-start.3
  46.2 7.3 %collective-permute-start.2 = (bf16[1024,384]{0,1:T(8,128)(2,1)}, bf16[1024,384]{0,1:T(8,128)(2,1)}, u32[]{:S(2)}, u32[]{:S(2)}) collective-permute-start(bf16[1024,384]{0,1:T(8,128)(2,1)} %get-tuple-element.6), channel_id=1, source_target_pairs={{0,2},{1,3},{2,4},{3,5},{4,6},{5,7},{6,8},{7,9},{8,10},{9,11},{10,... | collective-permute-start | bytes 2359304 | tf_op jit(solution)/shard_map/ppermute | solution.py:14
  53.8 15.1 %collective-permute-done.3 = bf16[1024,384]{0,1:T(8,128)(2,1)} collective-permute-done((bf16[1024,384]{0,1:T(8,128)(2,1)}, bf16[1024,384]{0,1:T(8,128)(2,1)}, u32[]{:S(2)}, u32[]{:S(2)}) %collective-permute-start.3) | collective-permute-done | bytes 786464 | tf_op jit(solution)/shard_map/ppermute | solution.py:14
  68.9 17.0 %collective-permute-done.2 = bf16[1024,384]{0,1:T(8,128)(2,1)} collective-permute-done((bf16[1024,384]{0,1:T(8,128)(2,1)}, bf16[1024,384]{0,1:T(8,128)(2,1)}, u32[]{:S(2)}, u32[]{:S(2)}) %collective-permute-start.2) | collective-permute-done | bytes 786464 | tf_op jit(solution)/shard_map/ppermute | solution.py:14
  85.9 3.7 %fusion = bf16[1024,384]{0,1:T(8,128)(2,1)S(1)} fusion(bf16[1024,384]{0,1:T(8,128)(2,1)S(1)} %copy.5, bf16[1024,384]{0,1:T(8,128)(2,1)} %collective-permute-done.3, bf16[1024,384]{0,1:T(8,128)(2,1)} %get-tuple-element.6, bf16[1024,384]{0,1:T(8,128)(2,1)} %collective-permute-done.2, bf16[2304,384]{1,0:T(8,128)(2,1)S(1)} %copy-done.1), kind=kOutput, calls=%fused_computation.12 | convolution fusion | flops 920911872 | bytes 4816896 | tf_op jit(solution)/shard_map/dot_general | solution.py:66
  89.6 4.4 %collective-permute-start.5 = (bf16[1024,384]{0,1:T(8,128)(2,1)S(1)}, bf16[1024,384]{0,1:T(8,128)(2,1)S(1)}, u32[]{:S(2)}, u32[]{:S(2)}) collective-permute-start(bf16[1024,384]{0,1:T(8,128)(2,1)S(1)} %fusion), channel_id=1, source_target_pairs={{0,2},{1,3},{2,4},{3,5},{4,6},{5,7},{6,8},{7,9},{8,10},{9,11},{10,... | collective-permute-start | bytes 2359304 | tf_op jit(solution)/shard_map/ppermute | solution.py:14
  94.0 1.3 collective-permute-start.4
  95.5 3.0 %convolution_multiply_fusion = f32[1152,384]{1,0:T(8,128)S(1)} fusion(bf16[1024,384]{0,1:T(8,128)(2,1)S(1)} %fusion, bf16[1024,384]{0,1:T(8,128)(2,1)} %collective-permute-done.3, bf16[1024,384]{0,1:T(8,128)(2,1)} %get-tuple-element.6, bf16[1024,384]{0,1:T(8,128)(2,1)} %collective-permute-done.2), kind=kOutput, calls=%fused_computation.1 | convolution fusion | flops 913489920 | bytes 4915200 | tf_op jit(solution)/shard_map/dot_general | solution.py:36
  98.6 29.3 %collective-permute-done.5 = bf16[1024,384]{0,1:T(8,128)(2,1)S(1)} collective-permute-done((bf16[1024,384]{0,1:T(8,128)(2,1)S(1)}, bf16[1024,384]{0,1:T(8,128)(2,1)S(1)}, u32[]{:S(2)}, u32[]{:S(2)}) %collective-permute-start.5) | collective-permute-done | bytes 786464 | tf_op jit(solution)/shard_map/ppermute | solution.py:14
  128.1 3.0 %fusion.12 = (bf16[1024,384]{0,1:T(8,128)(2,1)S(1)}, f32[1024,384]{0,1:T(8,128)}) fusion(f32[1024,384]{0,1:T(8,128)S(1)} %copy-done.4, bf16[3,384,384]{2,1,0:T(8,128)(2,1)S(1)} %bitcast.21, bf16[1024,3,384]{0,2,1:T(8,128)(2,1)S(1)} %bitcast.18, bf16[1024,384]{0,1:T(8,128)(2,1)S(1)} %copy.5), kind=kOutput, calls=%fused_computation.24 | convolution fusion | flops 914227200 | bytes 7962624 | tf_op jit(solution)/shard_map/dot_general | solution.py:30
  131.1 3.1 %convolution_multiply_fusion.1 = f32[1152,384]{1,0:T(8,128)S(1)} fusion(bf16[1024,1152]{1,0:T(8,128)(2,1)} %constant_dynamic-update-slice_fusion, bf16[1024,384]{0,1:T(8,128)(2,1)S(1)} %get-tuple-element.8), kind=kOutput, calls=%fused_computation.2 | convolution fusion | flops 906412032 | bytes 4915200 | tf_op jit(solution)/shard_map/dot_general | solution.py:36
  134.2 2.0 pad_maximum_fusion
  136.3 1.3 collective-permute-start.7
  137.6 1.3 collective-permute-start.6
  138.9 39.1 %reduce-scatter.2.cloned.1.call-done = f32[576,384]{1,0:T(8,128)} async-done(((f32[2304,384]{1,0:T(8,128)}), f32[576,384]{1,0:T(8,128)}) %reduce-scatter.2.cloned.1.call-update) | async-done | bytes 884752 | tf_op jit(solution)/shard_map/reduce_scatter | solution.py:86
  179.5 1.2 fusion.13
  181.8 47.0 %all-reduce.2.cloned.1.call-done = f32[576,384]{1,0:T(8,128)} async-done(((f32[576,384]{1,0:T(8,128)}), f32[576,384]{1,0:T(8,128)}) %all-reduce.2.cloned.1.call-update) | async-done | bytes 884752 | tf_op jit(solution)/shard_map/psum | solution.py:85
  228.8 2.1 copy.18
  (28 shorter events, 7.0 us)
Async XLA Ops:
  7.2 6.9 %copy-start = (bf16[1024,384]{1,0:T(8,128)(2,1)S(1)}, bf16[1024,384]{1,0:T(8,128)(2,1)}, u32[]{:S(2)}) copy-start(bf16[1024,384]{1,0:T(8,128)(2,1)} %param.3) | copy-start | bytes 2359300
  7.2 32.8 %all-gather.2.cloned.1.call-start = ((), (), s32[]{:S(2)}) async-start(), calls=%async_computation.1 | async-start | bytes 2211840 | tf_op jit(solution)/shard_map/all_gather | solution.py:47
  7.9 170.1 %reduce-scatter.2.cloned.1.call-start = ((), (), s32[]{:S(2)}) async-start(), calls=%async_computation.2 | async-start | bytes 4423680 | tf_op jit(solution)/shard_map/reduce_scatter | solution.py:86
  8.0 5.1 %collective-permute-start = (bf16[1024,384]{1,0:T(8,128)(2,1)}, bf16[1024,384]{1,0:T(8,128)(2,1)S(1)}, u32[]{:S(2)}, u32[]{:S(2)}) collective-permute-start(bf16[1024,384]{1,0:T(8,128)(2,1)} %param.3), channel_id=1, source_target_pairs={{0,1},{1,2},{2,3},{3,4},{4,5},{5,6},{6,7},{7,8},{8,9},{9,10},{10,1... | collective-permute-start | bytes 2359304 | tf_op jit(solution)/shard_map/ppermute | solution.py:14
  10.4 6.4 %collective-permute-start.1 = (bf16[1024,384]{1,0:T(8,128)(2,1)}, bf16[1024,384]{1,0:T(8,128)(2,1)S(1)}, u32[]{:S(2)}, u32[]{:S(2)}) collective-permute-start(bf16[1024,384]{1,0:T(8,128)(2,1)} %param.3), channel_id=1, source_target_pairs={{1,0},{2,1},{3,2},{4,3},{5,4},{6,5},{7,6},{8,7},{9,8},{10,9},{11,1... | collective-permute-start | bytes 2359304 | tf_op jit(solution)/shard_map/ppermute | solution.py:14
  17.8 35.7 %copy-start.2 = (bf16[1024,384]{1,0:T(8,128)(2,1)S(1)}, bf16[1024,384]{1,0:T(8,128)(2,1)}, u32[]{:S(2)}) copy-start(bf16[1024,384]{1,0:T(8,128)(2,1)} %param.4) | copy-start | bytes 2359300
  40.0 46.0 %copy-start.1 = (bf16[2304,384]{1,0:T(8,128)(2,1)S(1)}, bf16[2304,384]{1,0:T(8,128)(2,1)}, u32[]{:S(2)}) copy-start(bf16[2304,384]{1,0:T(8,128)(2,1)} %all-gather.2.cloned.1.call-done) | copy-start | bytes 5308420
  44.9 24.0 %collective-permute-start.3 = (bf16[1024,384]{0,1:T(8,128)(2,1)}, bf16[1024,384]{0,1:T(8,128)(2,1)}, u32[]{:S(2)}, u32[]{:S(2)}) collective-permute-start(bf16[1024,384]{0,1:T(8,128)(2,1)} %get-tuple-element.6), channel_id=1, source_target_pairs={{2,0},{3,1},{4,2},{5,3},{6,4},{7,5},{8,6},{9,7},{10,8},{11,9},{12,... | collective-permute-start | bytes 2359304 | tf_op jit(solution)/shard_map/ppermute | solution.py:14
  46.2 39.7 %collective-permute-start.2 = (bf16[1024,384]{0,1:T(8,128)(2,1)}, bf16[1024,384]{0,1:T(8,128)(2,1)}, u32[]{:S(2)}, u32[]{:S(2)}) collective-permute-start(bf16[1024,384]{0,1:T(8,128)(2,1)} %get-tuple-element.6), channel_id=1, source_target_pairs={{0,2},{1,3},{2,4},{3,5},{4,6},{5,7},{6,8},{7,9},{8,10},{9,11},{10,... | collective-permute-start | bytes 2359304 | tf_op jit(solution)/shard_map/ppermute | solution.py:14
  89.6 38.2 %collective-permute-start.5 = (bf16[1024,384]{0,1:T(8,128)(2,1)S(1)}, bf16[1024,384]{0,1:T(8,128)(2,1)S(1)}, u32[]{:S(2)}, u32[]{:S(2)}) collective-permute-start(bf16[1024,384]{0,1:T(8,128)(2,1)S(1)} %fusion), channel_id=1, source_target_pairs={{0,2},{1,3},{2,4},{3,5},{4,6},{5,7},{6,8},{7,9},{8,10},{9,11},{10,... | collective-permute-start | bytes 2359304 | tf_op jit(solution)/shard_map/ppermute | solution.py:14
  94.0 33.8 %collective-permute-start.4 = (bf16[1024,384]{0,1:T(8,128)(2,1)S(1)}, bf16[1024,384]{0,1:T(8,128)(2,1)S(1)}, u32[]{:S(2)}, u32[]{:S(2)}) collective-permute-start(bf16[1024,384]{0,1:T(8,128)(2,1)S(1)} %fusion), channel_id=1, source_target_pairs={{2,0},{3,1},{4,2},{5,3},{6,4},{7,5},{8,6},{9,7},{10,8},{11,9},{12,... | collective-permute-start | bytes 2359304 | tf_op jit(solution)/shard_map/ppermute | solution.py:14
  98.6 29.5 %copy-start.4 = (f32[1024,384]{0,1:T(8,128)S(1)}, f32[1024,384]{0,1:T(8,128)}, u32[]{:S(2)}) copy-start(f32[1024,384]{0,1:T(8,128)} %get-tuple-element.7) | copy-start | bytes 4718596
  136.2 92.6 %all-reduce.2.cloned.1.call-start = ((), (), s32[]{:S(2)}) async-start(), calls=%async_computation.3 | async-start | bytes 1769472 | tf_op jit(solution)/shard_map/psum | solution.py:85
  136.3 41.8 %collective-permute-start.7 = (bf16[1024,384]{0,1:T(8,128)(2,1)S(1)}, bf16[1024,384]{0,1:T(8,128)(2,1)S(1)}, u32[]{:S(2)}, u32[]{:S(2)}) collective-permute-start(bf16[1024,384]{0,1:T(8,128)(2,1)S(1)} %get-tuple-element.8), channel_id=1, source_target_pairs={{0,1},{1,2},{2,3},{3,4},{4,5},{5,6},{6,7},{7,8},{8,9},{9,10},{10,1... | collective-permute-start | bytes 2359304 | tf_op jit(solution)/shard_map/ppermute | solution.py:14
  137.6 40.5 %collective-permute-start.6 = (bf16[1024,384]{0,1:T(8,128)(2,1)S(1)}, bf16[1024,384]{0,1:T(8,128)(2,1)S(1)}, u32[]{:S(2)}, u32[]{:S(2)}) collective-permute-start(bf16[1024,384]{0,1:T(8,128)(2,1)S(1)} %get-tuple-element.8), channel_id=1, source_target_pairs={{1,0},{2,1},{3,2},{4,3},{5,4},{6,5},{7,6},{8,7},{9,8},{10,9},{11,1... | collective-permute-start | bytes 2359304 | tf_op jit(solution)/shard_map/ppermute | solution.py:14
  178.1 1.4 copy-start.3
Sparse Core Ops, SparseCore 0:
  9.6 30.3 all-gather.1
  136.3 41.6 reduce-scatter.1
  180.5 48.2 all-reduce.1
where the time goes:
time: 238 us; the launch traced here: 237 us
  waiting for transfers between devices  172 us (72%)
  starting transfers between devices  20.8 us (9%)
  matrix products  18.9 us (8%)
  between operations  13.9 us (6%)
  local copies, waits for them, and re-layouts  9.33 us (4%)
  other arithmetic  2.4 us (1%)
    ppermute x8, waiting for transfers between devices, from_behind(): return lax.ppermute(block, axis, route)  63.1 us
    psum x1, waiting for transfers between devices, per_device(): summed = lax.psum(local_grads, 'seq')  47 us
    reduce_scatter x1, waiting for transfers between devices, per_device(): lax.psum_scatter(summed, 'sub', scatter_dimension=0, tiled=True)  39.1 us
    all_gather x1, waiting for transfers between devices, per_device(): all_weights = lax.all_gather(weights, 'sub', axis=0, tiled=True)  22.2 us
    ppermute x8, starting transfers between devices, from_behind(): return lax.ppermute(block, axis, route)  20.7 us
    unnamed x16, local copies, waits for them, and re-layouts  8.17 us
    dot_general x2, matrix products, tap_grads(): lax.dot_general(stacked, delta, (((0,), (0,)), ((), ())), preferred_eleme...  6.12 us
    dot_general x1, matrix products, per_device(): jnp.dot(first_layer_weights, first, preferred_element_type=jnp.float32)  4.94 us
  transfers between devices with their start and end apart: 11, of which 7 were waited for; matrix products, arithmetic and copies ran while one was open for 4% of the time, Pallas kernels for 0%

commit v1 on v0

--- a/solution.py
+++ b/solution.py
@@ -1,11 +1,24 @@
+import functools
 import math
 import jax
 import jax.numpy as jnp
 from jax import lax
 from jax.sharding import PartitionSpec as P
+from jax.lax import axis_size, ppermute
 
 DILATION_FIRST = 1024
 DILATION_SECOND = 2048
+
+
+def part_unit(frame_in, axis_id):
+    carry = frame_in
+    p_count = axis_size(axis_id)
+    for ix in [[(b, b ^ c) for b in range(p_count)] for c in (1, 2, 4, 8, 16) if c < p_count]:
+        carry = carry + ppermute(carry, axis_id, ix)
+    return carry
+
+
+wrap_the_lines = functools.partial(part_unit, axis_id="seq")
 
 
 def from_behind(block, axis, distance):
@@ -82,7 +95,7 @@
         jnp.bfloat16
     )
     local_grads = jnp.concatenate((grad_one, grad_two), 0)
-    summed = lax.psum(local_grads, "seq")
+    summed = wrap_the_lines(local_grads)
     weight_grad = lax.psum_scatter(summed, "sub", scatter_dimension=0, tiled=True)
     return (input_grad, weight_grad)
 

time: 238 us -> 419 us (1.76)
  waiting for transfers between devices: 172 us -> 349 us
  starting transfers between devices: 20.8 us -> 26.2 us
    ppermute x0 -> x2, waiting for transfers between devices: none -> 229 us  [part_unit(): carry = carry + ppermute(carry, axis_id, ix)]
    psum x1 -> x0, waiting for transfers between devices: 47 us -> none  [per_device(): summed = lax.psum(local_grads, 'seq')]
    reduce_scatter x1, waiting for transfers between devices: 39.1 us -> 31.5 us  [per_device(): lax.psum_scatter(summed, 'sub', scatter_dimension=0, tiled=True)]
    ppermute x0 -> x2, starting transfers between devices: none -> 5.38 us  [part_unit(): carry = carry + ppermute(carry, axis_id, ix)]
  transfers between devices with their start and end apart: 11 -> 12, of which waited for: 7 -> 10; matrix products, arithmetic and copies ran while one was open for 4% -> 3% of each run, Pallas kernels for 0% -> 0%
where the time goes in v1:
time: 419 us; the launch traced here: 418 us
  waiting for transfers between devices  349 us (83%)
  starting transfers between devices  26.2 us (6%)
  matrix products  19 us (5%)
  between operations  14.2 us (3%)
  local copies, waits for them, and re-layouts  6.08 us (1%)
    ppermute x2, waiting for transfers between devices, part_unit(): carry = carry + ppermute(carry, axis_id, ix)  229 us
    ppermute x8, waiting for transfers between devices, from_behind(): return lax.ppermute(block, axis, route)  66 us
    reduce_scatter x1, waiting for transfers between devices, per_device(): lax.psum_scatter(summed, 'sub', scatter_dimension=0, tiled=True)  31.5 us
    all_gather x1, waiting for transfers between devices, per_device(): all_weights = lax.all_gather(weights, 'sub', axis=0, tiled=True)  22.1 us
    ppermute x8, starting transfers between devices, from_behind(): return lax.ppermute(block, axis, route)  20.8 us
  transfers between devices with their start and end apart: 12, of which 10 were waited for; matrix products, arithmetic and copies ran while one was open for 3% of the time, Pallas kernels for 0%

profile of v1, /device:TPU:0, one launch (start us, length us, event | category | flops | bytes accessed | tf_op | source)
XLA Modules:
  0.0 417.6 jit_solution(17546827383203897463)
XLA Ops:
  8.0 2.4 collective-permute-start
  10.4 1.3 collective-permute-start.1
  11.7 1.4 copy.6
  15.1 1.7 collective-permute-done.1
  17.8 22.1 %all-gather.2.cloned.1.call-done = bf16[2304,384]{1,0:T(8,128)(2,1)} async-done(((bf16[576,384]{1,0:T(8,128)(2,1)}), bf16[2304,384]{1,0:T(8,128)(2,1)}) %all-gather.2.cloned.1.call-update) | async-done | bytes 1769488 | tf_op jit(solution)/shard_map/all_gather | solution.py:60
  40.0 4.9 %add_convert_fusion = (bf16[1024,384]{0,1:T(8,128)(2,1)}, f32[1024,384]{0,1:T(8,128)}) fusion(bf16[1024,384]{0,1:T(8,128)(2,1)S(1)} %copy.6, bf16[1024,1152]{1,0:T(8,128)(2,1)} %constant_dynamic-update-slice_fusion, bf16[2304,384]{1,0:T(8,128)(2,1)} %all-gather.2.cloned.1.call-done), kind=kOutput, calls=%fused_computation.27 | convolution fusion | flops 910295040 | bytes 6389760 | tf_op jit(solution)/shard_map/dot_general | solution.py:73
  46.2 7.3 %collective-permute-start.2 = (bf16[1024,384]{0,1:T(8,128)(2,1)}, bf16[1024,384]{0,1:T(8,128)(2,1)}, u32[]{:S(2)}, u32[]{:S(2)}) collective-permute-start(bf16[1024,384]{0,1:T(8,128)(2,1)} %get-tuple-element.6), channel_id=1, source_target_pairs={{0,2},{1,3},{2,4},{3,5},{4,6},{5,7},{6,8},{7,9},{8,10},{9,11},{10,... | collective-permute-start | bytes 2359304 | tf_op jit(solution)/shard_map/ppermute | solution.py:27
  53.8 15.1 %collective-permute-done.3 = bf16[1024,384]{0,1:T(8,128)(2,1)} collective-permute-done((bf16[1024,384]{0,1:T(8,128)(2,1)}, bf16[1024,384]{0,1:T(8,128)(2,1)}, u32[]{:S(2)}, u32[]{:S(2)}) %collective-permute-start.3) | collective-permute-done | bytes 786464 | tf_op jit(solution)/shard_map/ppermute | solution.py:27
  68.9 17.0 %collective-permute-done.2 = bf16[1024,384]{0,1:T(8,128)(2,1)} collective-permute-done((bf16[1024,384]{0,1:T(8,128)(2,1)}, bf16[1024,384]{0,1:T(8,128)(2,1)}, u32[]{:S(2)}, u32[]{:S(2)}) %collective-permute-start.2) | collective-permute-done | bytes 786464 | tf_op jit(solution)/shard_map/ppermute | solution.py:27
  85.9 3.7 fusion
  89.6 4.4 %collective-permute-start.5 = (bf16[1024,384]{0,1:T(8,128)(2,1)S(1)}, bf16[1024,384]{0,1:T(8,128)(2,1)S(1)}, u32[]{:S(2)}, u32[]{:S(2)}) collective-permute-start(bf16[1024,384]{0,1:T(8,128)(2,1)S(1)} %fusion), channel_id=1, source_target_pairs={{0,2},{1,3},{2,4},{3,5},{4,6},{5,7},{6,8},{7,9},{8,10},{9,11},{10,... | collective-permute-start | bytes 2359304 | tf_op jit(solution)/shard_map/ppermute | solution.py:27
  94.0 1.3 collective-permute-start.4
  95.5 3.0 convolution_multiply_fusion
  98.6 29.3 %collective-permute-done.5 = bf16[1024,384]{0,1:T(8,128)(2,1)S(1)} collective-permute-done((bf16[1024,384]{0,1:T(8,128)(2,1)S(1)}, bf16[1024,384]{0,1:T(8,128)(2,1)S(1)}, u32[]{:S(2)}, u32[]{:S(2)}) %collective-permute-start.5) | collective-permute-done | bytes 786464 | tf_op jit(solution)/shard_map/ppermute | solution.py:27
  128.1 3.1 fusion.12
  131.1 3.1 convolution_multiply_fusion.1
  134.5 2.6 collective-permute-start.8
  137.0 76.7 %collective-permute-done.8 = f32[2304,384]{1,0:T(8,128)S(1)} collective-permute-done((f32[2304,384]{1,0:T(8,128)S(1)}, f32[2304,384]{1,0:T(8,128)S(1)}, u32[]{:S(2)}, u32[]{:S(2)}) %collective-permute-start.8) | collective-permute-done | bytes 3538976 | tf_op jit(solution)/shard_map/ppermute | solution.py:17
  214.1 2.8 collective-permute-start.9
  216.9 151.9 %collective-permute-done.9 = f32[2304,384]{1,0:T(8,128)S(1)} collective-permute-done((f32[2304,384]{1,0:T(8,128)S(1)}, f32[2304,384]{1,0:T(8,128)S(1)}, u32[]{:S(2)}, u32[]{:S(2)}) %collective-permute-start.9) | collective-permute-done | bytes 3538976 | tf_op jit(solution)/shard_map/ppermute | solution.py:17
  368.8 2.1 add.54
  371.0 1.5 collective-permute-start.7
  374.3 2.3 collective-permute-done.6
  379.2 31.5 %reduce-scatter.2.cloned.1.call-done = f32[576,384]{1,0:T(8,128)} async-done(((f32[2304,384]{1,0:T(8,128)}), f32[576,384]{1,0:T(8,128)}) %reduce-scatter.2.cloned.1.call-update) | async-done | bytes 884752 | tf_op jit(solution)/shard_map/reduce_scatter | solution.py:99
  (30 shorter events, 10.7 us)
Async XLA Ops:
  7.2 6.9 %copy-start = (bf16[1024,384]{1,0:T(8,128)(2,1)S(1)}, bf16[1024,384]{1,0:T(8,128)(2,1)}, u32[]{:S(2)}) copy-start(bf16[1024,384]{1,0:T(8,128)(2,1)} %param.3) | copy-start | bytes 2359300
  7.2 32.8 %all-gather.2.cloned.1.call-start = ((), (), s32[]{:S(2)}) async-start(), calls=%async_computation.1 | async-start | bytes 2211840 | tf_op jit(solution)/shard_map/all_gather | solution.py:60
  7.9 402.8 %reduce-scatter.2.cloned.1.call-start = ((), (), s32[]{:S(2)}) async-start(), calls=%async_computation.2 | async-start | bytes 4423680 | tf_op jit(solution)/shard_map/reduce_scatter | solution.py:99
  8.0 5.1 %collective-permute-start = (bf16[1024,384]{1,0:T(8,128)(2,1)}, bf16[1024,384]{1,0:T(8,128)(2,1)S(1)}, u32[]{:S(2)}, u32[]{:S(2)}) collective-permute-start(bf16[1024,384]{1,0:T(8,128)(2,1)} %param.3), channel_id=1, source_target_pairs={{0,1},{1,2},{2,3},{3,4},{4,5},{5,6},{6,7},{7,8},{8,9},{9,10},{10,1... | collective-permute-start | bytes 2359304 | tf_op jit(solution)/shard_map/ppermute | solution.py:27
  10.4 6.4 %collective-permute-start.1 = (bf16[1024,384]{1,0:T(8,128)(2,1)}, bf16[1024,384]{1,0:T(8,128)(2,1)S(1)}, u32[]{:S(2)}, u32[]{:S(2)}) collective-permute-start(bf16[1024,384]{1,0:T(8,128)(2,1)} %param.3), channel_id=1, source_target_pairs={{1,0},{2,1},{3,2},{4,3},{5,4},{6,5},{7,6},{8,7},{9,8},{10,9},{11,1... | collective-permute-start | bytes 2359304 | tf_op jit(solution)/shard_map/ppermute | solution.py:27
  17.8 35.6 %copy-start.2 = (bf16[1024,384]{1,0:T(8,128)(2,1)S(1)}, bf16[1024,384]{1,0:T(8,128)(2,1)}, u32[]{:S(2)}) copy-start(bf16[1024,384]{1,0:T(8,128)(2,1)} %param.4) | copy-start | bytes 2359300
  39.9 46.0 %copy-start.1 = (bf16[2304,384]{1,0:T(8,128)(2,1)S(1)}, bf16[2304,384]{1,0:T(8,128)(2,1)}, u32[]{:S(2)}) copy-start(bf16[2304,384]{1,0:T(8,128)(2,1)} %all-gather.2.cloned.1.call-done) | copy-start | bytes 5308420
  44.9 24.0 %collective-permute-start.3 = (bf16[1024,384]{0,1:T(8,128)(2,1)}, bf16[1024,384]{0,1:T(8,128)(2,1)}, u32[]{:S(2)}, u32[]{:S(2)}) collective-permute-start(bf16[1024,384]{0,1:T(8,128)(2,1)} %get-tuple-element.6), channel_id=1, source_target_pairs={{2,0},{3,1},{4,2},{5,3},{6,4},{7,5},{8,6},{9,7},{10,8},{11,9},{12,... | collective-permute-start | bytes 2359304 | tf_op jit(solution)/shard_map/ppermute | solution.py:27
  46.2 39.7 %collective-permute-start.2 = (bf16[1024,384]{0,1:T(8,128)(2,1)}, bf16[1024,384]{0,1:T(8,128)(2,1)}, u32[]{:S(2)}, u32[]{:S(2)}) collective-permute-start(bf16[1024,384]{0,1:T(8,128)(2,1)} %get-tuple-element.6), channel_id=1, source_target_pairs={{0,2},{1,3},{2,4},{3,5},{4,6},{5,7},{6,8},{7,9},{8,10},{9,11},{10,... | collective-permute-start | bytes 2359304 | tf_op jit(solution)/shard_map/ppermute | solution.py:27
  89.6 38.2 %collective-permute-start.5 = (bf16[1024,384]{0,1:T(8,128)(2,1)S(1)}, bf16[1024,384]{0,1:T(8,128)(2,1)S(1)}, u32[]{:S(2)}, u32[]{:S(2)}) collective-permute-start(bf16[1024,384]{0,1:T(8,128)(2,1)S(1)} %fusion), channel_id=1, source_target_pairs={{0,2},{1,3},{2,4},{3,5},{4,6},{5,7},{6,8},{7,9},{8,10},{9,11},{10,... | collective-permute-start | bytes 2359304 | tf_op jit(solution)/shard_map/ppermute | solution.py:27
  94.0 33.8 %collective-permute-start.4 = (bf16[1024,384]{0,1:T(8,128)(2,1)S(1)}, bf16[1024,384]{0,1:T(8,128)(2,1)S(1)}, u32[]{:S(2)}, u32[]{:S(2)}) collective-permute-start(bf16[1024,384]{0,1:T(8,128)(2,1)S(1)} %fusion), channel_id=1, source_target_pairs={{2,0},{3,1},{4,2},{5,3},{6,4},{7,5},{8,6},{9,7},{10,8},{11,9},{12,... | collective-permute-start | bytes 2359304 | tf_op jit(solution)/shard_map/ppermute | solution.py:27
  98.6 29.5 %copy-start.4 = (f32[1024,384]{0,1:T(8,128)S(1)}, f32[1024,384]{0,1:T(8,128)}, u32[]{:S(2)}) copy-start(f32[1024,384]{0,1:T(8,128)} %get-tuple-element.7) | copy-start | bytes 4718596
  134.5 79.3 %collective-permute-start.8 = (f32[2304,384]{1,0:T(8,128)S(1)}, f32[2304,384]{1,0:T(8,128)S(1)}, u32[]{:S(2)}, u32[]{:S(2)}) collective-permute-start(f32[2304,384]{1,0:T(8,128)S(1)} %pad_maximum_fusion), channel_id=1, source_target_pairs={{0,4},{4,0},{8,12},{12,8},{1,5},{5,1},{9,13},{13,9},{2,6},{6,2},{1... | collective-permute-start | bytes 10616840 | tf_op jit(solution)/shard_map/ppermute | solution.py:17
  214.1 154.7 %collective-permute-start.9 = (f32[2304,384]{1,0:T(8,128)S(1)}, f32[2304,384]{1,0:T(8,128)S(1)}, u32[]{:S(2)}, u32[]{:S(2)}) collective-permute-start(f32[2304,384]{1,0:T(8,128)S(1)} %fusion.20), channel_id=1, source_target_pairs={{0,8},{4,12},{8,0},{12,4},{1,9},{5,13},{9,1},{13,5},{2,10},{6,14},... | collective-permute-start | bytes 10616840 | tf_op jit(solution)/shard_map/ppermute | solution.py:17
  371.0 5.9 %copy-start.3 = (f32[1024,384]{0,1:T(8,128)S(1)}, f32[1024,384]{0,1:T(8,128)}, u32[]{:S(2)}) copy-start(f32[1024,384]{0,1:T(8,128)} %get-tuple-element.9) | copy-start | bytes 4718596
  371.0 3.3 collective-permute-start.7
  372.5 4.2 %collective-permute-start.6 = (bf16[1024,384]{0,1:T(8,128)(2,1)S(1)}, bf16[1024,384]{0,1:T(8,128)(2,1)S(1)}, u32[]{:S(2)}, u32[]{:S(2)}) collective-permute-start(bf16[1024,384]{0,1:T(8,128)(2,1)S(1)} %get-tuple-element.8), channel_id=1, source_target_pairs={{1,0},{2,1},{3,2},{4,3},{5,4},{6,5},{7,6},{8,7},{9,8},{10,9},{11,1... | collective-permute-start | bytes 2359304 | tf_op jit(solution)/shard_map/ppermute | solution.py:27
Sparse Core Ops, SparseCore 0:
  9.6 30.3 all-gather.1
  371.1 39.6 reduce-scatter.1
